TPU v7x, 256 devices: a whole 4x4x8 slice. The times are simulated.
256 devices in a mesh: grp: 4 (over y_lo, core), trk: 64 (over z, x, y_hi).
Axes of the slice: x: 4, y: 4 (y_hi: 2, y_lo: 2; y = y_hi * 2 + y_lo), z: 8, core: 2. Of those that a mesh axis runs over, the one named last changes fastest.
Arguments:
- fields: bfloat16 [256, 512, 512], P('grp', 'trk'), may hold values from -81 to 81
- upstream: bfloat16 [256, 512, 512], P('grp', 'trk'), may hold values from -6 to 6
- ln_gain: float32 [512], replicated, may hold values from 0.1 to 1.9
- weights: bfloat16 [4, 512, 512], P(None, 'grp', 'trk'), may hold values from -8 to 8
Outputs:
- grad_fields: bfloat16 [256, 512, 512], P('grp', 'trk')
- grad_weights: float32 [4, 512, 512], P(None, 'grp', 'trk')
- grad_gain: float32 [512], replicated
All inputs are finite; a program needn't handle non-finite values.
Results may differ from a plain program's by a relative error of at most 0.014.
The roundings to bfloat16 on the way count: a program that leaves them out, or rounds other values in their place, can miss the bound.
Values may be sent and summed in bfloat16 or wider, within the bound.
A program may use at most 64 MiB of HBM per device.

v0:
```python
import jax
import jax.numpy as jnp
from jax import lax
from jax.sharding import PartitionSpec as P

HEADS = 8


def normalize(fields, ln_gain):
    values = fields.astype(jnp.float32)
    row_mean = jnp.mean(values, -1, keepdims=True)
    offset = values - row_mean
    row_var = jnp.mean(offset * offset, -1, keepdims=True)
    inv_std = lax.rsqrt(row_var + 1e-05)
    centred = offset * inv_std
    normed = (centred * ln_gain).astype(jnp.bfloat16)
    return (normed, centred, inv_std)


def project(normed, w_in):
    return [
        jnp.einsum("rti,ij->rtj", normed, w_in[index], preferred_element_type=jnp.float32).astype(
            jnp.bfloat16
        )
        for index in range(3)
    ]


def split_heads(block, heads):
    rows, length, width = block.shape
    return (
        block.reshape(rows, length, heads, width // heads)
        .transpose(0, 2, 1, 3)
        .reshape(rows * heads, length, width // heads)
    )


def merge_heads(block, rows):
    items, length, size = block.shape
    return (
        block.reshape(rows, items // rows, length, size)
        .transpose(0, 2, 1, 3)
        .reshape(rows, length, items // rows * size)
    )


def head_back(members):
    query, keyed, valued, grad_out = members
    scaling = query.shape[-1] ** (-0.5)
    scores = jnp.einsum("qd,kd->qk", query, keyed, preferred_element_type=jnp.float32) * scaling
    row_max = jnp.max(scores, -1, keepdims=True)
    shifted = jnp.exp(scores - row_max)
    attn_prob = shifted / jnp.sum(shifted, -1, keepdims=True)
    prob_low = attn_prob.astype(jnp.bfloat16)
    output = jnp.einsum("qk,kd->qd", prob_low, valued, preferred_element_type=jnp.float32).astype(
        jnp.bfloat16
    )
    dprobs = jnp.einsum("qd,kd->qk", grad_out, valued, preferred_element_type=jnp.float32)
    row_dot = jnp.sum(attn_prob * dprobs, -1, keepdims=True)
    score_grad = (attn_prob * (dprobs - row_dot) * scaling).astype(jnp.bfloat16)
    grad_value = jnp.einsum(
        "qk,qd->kd", prob_low, grad_out, preferred_element_type=jnp.float32
    ).astype(jnp.bfloat16)
    grad_query = jnp.einsum(
        "qk,kd->qd", score_grad, keyed, preferred_element_type=jnp.float32
    ).astype(jnp.bfloat16)
    grad_key = jnp.einsum(
        "qk,qd->kd", score_grad, query, preferred_element_type=jnp.float32
    ).astype(jnp.bfloat16)
    return (output, grad_query, grad_key, grad_value)


def attend_back(query_proj, key_proj, value_proj, upstream_rows, w_out):
    rows = query_proj.shape[0]
    grad_attended = jnp.einsum(
        "rtj,ij->rti", upstream_rows, w_out, preferred_element_type=jnp.float32
    ).astype(jnp.bfloat16)
    pieces = lax.map(
        head_back,
        (
            split_heads(query_proj, HEADS),
            split_heads(key_proj, HEADS),
            split_heads(value_proj, HEADS),
            split_heads(grad_attended, HEADS),
        ),
    )
    return [merge_heads(piece, rows) for piece in pieces]


def input_grad(grad_query, grad_key, grad_value, w_in, centred, inv_std, ln_gain):
    stacked = jnp.stack([grad_query, grad_key, grad_value], 2)
    grad_normed = jnp.einsum("rtcj,cij->rti", stacked, w_in, preferred_element_type=jnp.float32)
    width = grad_normed.shape[-1]
    gain_term = jnp.sum((grad_normed * centred).reshape(-1, width), 0)
    scaled = grad_normed * ln_gain
    branch = inv_std * (
        scaled
        - jnp.mean(scaled, -1, keepdims=True)
        - centred * jnp.mean(scaled * centred, -1, keepdims=True)
    )
    return (branch.astype(jnp.bfloat16), gain_term)


def proj_grads(normed, grad_query, grad_key, grad_value):
    return [
        jnp.einsum("rti,rtj->ij", normed, member, preferred_element_type=jnp.float32)
        for member in (grad_query, grad_key, grad_value)
    ]


def shards(fields, upstream, ln_gain, weights):
    w_part = lax.all_gather(weights, "trk", axis=2, tiled=True)
    w_full = lax.all_gather(w_part, "grp", axis=1, tiled=True)
    w_in = w_full[:3]
    w_out = w_full[3]
    rows_dev, trk_dev, width = fields.shape
    cell_count = rows_dev * lax.axis_size("grp") * trk_dev * lax.axis_size("trk")
    normed, centred, inv_std = normalize(fields, ln_gain)
    query_proj, key_proj, value_proj = project(normed, w_in)
    query_rows, key_rows, value_rows, upstream_rows = (
        lax.all_to_all(query_proj, "trk", split_axis=0, concat_axis=1, tiled=True),
        lax.all_to_all(key_proj, "trk", split_axis=0, concat_axis=1, tiled=True),
        lax.all_to_all(value_proj, "trk", split_axis=0, concat_axis=1, tiled=True),
        lax.all_to_all(upstream, "trk", split_axis=0, concat_axis=1, tiled=True),
    )
    attended, grad_query, grad_key, grad_value = attend_back(
        query_rows, key_rows, value_rows, upstream_rows, w_out
    )
    back_query, back_key, back_value = (
        lax.all_to_all(grad_query, "trk", split_axis=1, concat_axis=0, tiled=True),
        lax.all_to_all(grad_key, "trk", split_axis=1, concat_axis=0, tiled=True),
        lax.all_to_all(grad_value, "trk", split_axis=1, concat_axis=0, tiled=True),
    )
    grad_list = proj_grads(normed, back_query, back_key, back_value)
    branch_cells, gain_term = input_grad(
        back_query, back_key, back_value, w_in, centred, inv_std, ln_gain
    )
    out_grad = jnp.einsum(
        "rti,rtj->ij", attended, upstream_rows, preferred_element_type=jnp.float32
    )
    raw_grad = jnp.stack(grad_list + [out_grad])
    partial_grad = lax.psum_scatter(
        raw_grad.astype(jnp.bfloat16), "grp", scatter_dimension=1, tiled=True
    ).astype(jnp.float32)
    summed_grad = lax.psum_scatter(partial_grad, "trk", scatter_dimension=2, tiled=True)
    gain_sum = lax.psum(gain_term, ("grp", "trk"))
    factor = float(cell_count) ** (-0.5)
    grad_fields = (upstream.astype(jnp.float32) + branch_cells.astype(jnp.float32)).astype(
        jnp.bfloat16
    )
    return (grad_fields, summed_grad * factor, gain_sum * factor)


def solution(mesh):
    in_specs = (P("grp", "trk", None), P("grp", "trk", None), P(), P(None, "grp", "trk"))
    out_specs = (P("grp", "trk", None), P(None, "grp", "trk"), P())
    return jax.shard_map(shards, mesh=mesh, in_specs=in_specs, out_specs=out_specs, check_vma=False)
```

profile of v0, /device:TPU:2, one launch (start us, length us, event | category | flops | bytes accessed | tf_op | source)
XLA Modules:
  0.0 1188.6 jit_solution(13073194801549360445)
XLA Ops:
  8.0 184.0 %all_gather.6 = bf16[4,128,512]{1,0,2:T(4,128)(2,1)S(1)} all-gather(bf16[4,128,8]{1,0,2:T(4,128)(2,1)S(1)} %copy.57), channel_id=1, replica_groups=mesh['grp'=4,'trk'=64] {'trk'}, dimensions={2}, use_global_device_ids=true | all-gather | bytes 532480 | tf_op jit(solution)/shard_map/all_gather | solution.py:112
  193.1 8.9 all-to-all-start.3
  202.5 21.9 %all-gather.2.cloned.1.call-done = bf16[4,512,512]{2,1,0:T(8,128)(2,1)} async-done(((bf16[4,128,512]{2,1,0:T(8,128)(2,1)}), bf16[4,512,512]{2,1,0:T(8,128)(2,1)}) %all-gather.2.cloned.1.call-update) | async-done | bytes 2097168 | tf_op jit(solution)/shard_map/all_gather | solution.py:113
  226.6 13.0 %all-to-all-start = ((bf16[64,8,512]{2,1,0:T(8,128)(2,1)}), bf16[64,8,512]{2,1,0:T(8,128)(2,1)S(1)}, u32[]{:S(2)}, u32[]{:S(2)}) async-start(bf16[64,8,512]{2,1,0:T(8,128)(2,1)} %convolution_convert_fusion.8), calls=%async_computation | async-start | bytes 1048576 | tf_op jit(solution)/shard_map/all_to_all | solution.py:121
  239.7 2.3 convolution_convert_fusion.7
  242.0 16.4 %all-to-all-done = bf16[64,8,512]{2,1,0:T(8,128)(2,1)S(1)} async-done(((bf16[64,8,512]{2,1,0:T(8,128)(2,1)}), bf16[64,8,512]{2,1,0:T(8,128)(2,1)S(1)}, u32[]{:S(2)}, u32[]{:S(2)}) %all-to-all-start) | async-done | bytes 524320 | tf_op jit(solution)/shard_map/all_to_all | solution.py:121
  258.4 6.5 all-to-all-start.1
  265.0 2.3 convolution_convert_fusion.6
  267.3 15.6 %all-to-all-done.1 = bf16[64,8,512]{2,1,0:T(8,128)(2,1)S(1)} async-done(((bf16[64,8,512]{2,1,0:T(8,128)(2,1)}), bf16[64,8,512]{2,1,0:T(8,128)(2,1)S(1)}, u32[]{:S(2)}, u32[]{:S(2)}) %all-to-all-start.1) | async-done | bytes 524320 | tf_op jit(solution)/shard_map/all_to_all | solution.py:122
  282.9 6.7 all-to-all-start.2
  293.1 2.4 reshape.122
  296.9 9.8 all-to-all-done.2
  306.7 2.4 reshape.124
  309.1 2.3 copy.62
  311.4 60.7 %while.16 = (s32[]{:T(128)}, bf16[8,512,64]{1,2,0:T(8,128)(2,1)}, bf16[8,512,64]{1,2,0:T(8,128)(2,1)}, bf16[8,512,64]{1,2,0:T(8,128)(2,1)}, bf16[8,512,64]{1,2,0...) while((s32[]{:T(128)}, bf16[8,512,64]{1,2,0:T(8,128)(2,1)}, ...), condition=%wide.region_6.7_spmd, body=%wide.region_2.6_spmd.sunk | while | flops 206699008 | bytes 11305061 | solution.py:78
  372.1 2.4 copy.65
  375.1 3.8 reduce.1
  379.9 6.5 all-to-all-start.6
  386.4 2.4 copy.64
  388.8 3.8 reduce.2
  393.6 9.5 all-to-all-done.6
  403.1 6.7 all-to-all-start.5
  409.8 2.4 copy.63
  412.2 3.8 reduce.3
  419.9 6.2 all-to-all-done.5
  426.1 6.6 all-to-all-start.4
  434.4 3.6 reshape.149
  439.5 8.9 all-to-all-done.4
  458.0 21.6 %reduce-scatter.2.cloned.1.call-done = bf16[4,128,512]{2,1,0:T(8,128)(2,1)} async-done(((bf16[4,512,512]{2,1,0:T(8,128)(2,1)}), bf16[4,128,512]{2,1,0:T(8,128)(2,1)}) %reduce-scatter.2.cloned.1.call-update) | async-done | bytes 524304 | tf_op jit(solution)/shard_map/reduce_scatter | solution.py:142
  481.9 2.8 fusion.64
  484.8 76.2 %psum.7 = f32[512]{0:T(512)S(1)} all-reduce(f32[512]{0:T(512)S(1)} %get-tuple-element.108), channel_id=1, replica_groups=mesh['grp'=4,'trk'=64] {'grp','trk'}, use_global_device_ids=true, to_apply=%region_12.13 | all-reduce | flops 512 | bytes 4096 | tf_op jit(solution)/shard_map/psum | solution.py:146
  562.8 617.9 %all-reduce.3.cloned.1.call-done = f32[4,128,512]{1,0,2:T(4,128)} async-done(((f32[4,128,512]{1,0,2:T(4,128)}), f32[4,128,512]{1,0,2:T(4,128)}) %all-reduce.3.cloned.1.call-update) | async-done | bytes 1048592
  (128 shorter events, 94.1 us)
Async XLA Ops:
  7.2 194.8 %copy-start = (bf16[64,8,512]{2,1,0:T(8,128)(2,1)S(1)}, bf16[64,8,512]{2,1,0:T(8,128)(2,1)}, u32[]{:S(2)}) copy-start(bf16[64,8,512]{2,1,0:T(8,128)(2,1)} %param.6) | copy-start | bytes 1572868
  7.2 217.1 %all-gather.2.cloned.1.call-start = ((), (), s32[]{:S(2)}) async-start(), calls=%async_computation.8 | async-start | bytes 2621440 | tf_op jit(solution)/shard_map/all_gather | solution.py:113
  8.0 216.3 %copy-start.8 = (f32[512]{0:T(512)S(1)}, f32[512]{0:T(512)}, u32[]{:S(2)}) copy-start(f32[512]{0:T(512)} %param.8) | copy-start | bytes 6148
  193.1 33.6 %all-to-all-start.3 = ((bf16[64,8,512]{2,1,0:T(8,128)(2,1)}), bf16[64,8,512]{2,1,0:T(8,128)(2,1)S(1)}, u32[]{:S(2)}, u32[]{:S(2)}) async-start(bf16[64,8,512]{2,1,0:T(8,128)(2,1)} %param.7), calls=%async_computation.3 | async-start | bytes 1048576 | tf_op jit(solution)/shard_map/all_to_all | solution.py:124
  226.6 31.8 %all-to-all-start = ((bf16[64,8,512]{2,1,0:T(8,128)(2,1)}), bf16[64,8,512]{2,1,0:T(8,128)(2,1)S(1)}, u32[]{:S(2)}, u32[]{:S(2)}) async-start(bf16[64,8,512]{2,1,0:T(8,128)(2,1)} %convolution_convert_fusion.8), calls=%async_computation | async-start | bytes 1048576 | tf_op jit(solution)/shard_map/all_to_all | solution.py:121
  258.4 24.4 %all-to-all-start.1 = ((bf16[64,8,512]{2,1,0:T(8,128)(2,1)}), bf16[64,8,512]{2,1,0:T(8,128)(2,1)S(1)}, u32[]{:S(2)}, u32[]{:S(2)}) async-start(bf16[64,8,512]{2,1,0:T(8,128)(2,1)} %convolution_convert_fusion.7), calls=%async_computation.1 | async-start | bytes 1048576 | tf_op jit(solution)/shard_map/all_to_all | solution.py:122
  282.9 9.6 copy-start.2
  282.9 23.8 %all-to-all-start.2 = ((bf16[64,8,512]{2,1,0:T(8,128)(2,1)}), bf16[64,8,512]{2,1,0:T(8,128)(2,1)}, u32[]{:S(2)}, u32[]{:S(2)}) async-start(bf16[64,8,512]{2,1,0:T(8,128)(2,1)} %convolution_convert_fusion.6), calls=%async_computation.2 | async-start | bytes 1048576 | tf_op jit(solution)/shard_map/all_to_all | solution.py:123
  379.9 23.2 %all-to-all-start.6 = ((bf16[64,2,2048]{2,1,0:T(2,128)(2,1)}), bf16[64,2,2048]{2,1,0:T(2,128)(2,1)S(1)}, u32[]{:S(2)}, u32[]{:S(2)}) async-start(bf16[64,2,2048]{2,1,0:T(2,128)(2,1)} %reshape.146), calls=%async_computation.6 | async-start | bytes 1048576 | tf_op jit(solution)/shard_map/all_to_all | solution.py:132
  403.1 22.9 %all-to-all-start.5 = ((bf16[64,2,2048]{2,1,0:T(2,128)(2,1)}), bf16[64,2,2048]{2,1,0:T(2,128)(2,1)}, u32[]{:S(2)}, u32[]{:S(2)}) async-start(bf16[64,2,2048]{2,1,0:T(2,128)(2,1)} %reshape.148), calls=%async_computation.5 | async-start | bytes 1048576 | tf_op jit(solution)/shard_map/all_to_all | solution.py:131
  426.1 22.4 %all-to-all-start.4 = ((bf16[64,2,2048]{2,1,0:T(2,128)(2,1)}), bf16[64,2,2048]{2,1,0:T(2,128)(2,1)S(1)}, u32[]{:S(2)}, u32[]{:S(2)}) async-start(bf16[64,2,2048]{2,1,0:T(2,128)(2,1)} %reshape.150), calls=%async_computation.4 | async-start | bytes 1048576 | tf_op jit(solution)/shard_map/all_to_all | solution.py:130
  432.6 47.0 %reduce-scatter.2.cloned.1.call-start = ((), (), s32[]{:S(2)}) async-start(), calls=%async_computation.9 | async-start | bytes 2621440 | tf_op jit(solution)/shard_map/reduce_scatter | solution.py:142
  450.2 2.0 copy-start.4
  450.2 2.0 copy-start.6
  450.2 2.0 copy-start.7
  453.9 0.7 copy-start.9
  453.9 726.9 %all-reduce.3.cloned.1.call-start = ((), (), s32[]{:S(2)}) async-start(), calls=%async_computation.10 | async-start | bytes 2097152
  455.8 1.3 copy-start.1
  457.1 24.8 %copy-start.5 = (bf16[1,512,512]{2,1,0:T(8,128)(2,1)S(1)}, bf16[1,512,512]{2,1,0:T(8,128)(2,1)}, u32[]{:S(2)}) copy-start(bf16[1,512,512]{2,1,0:T(8,128)(2,1)} %copy.94) | copy-start | bytes 1572868
  481.9 79.7 %copy-start.3 = (bf16[64,8,512]{2,1,0:T(8,128)(2,1)S(1)}, bf16[64,8,512]{2,1,0:T(8,128)(2,1)}, u32[]{:S(2)}) copy-start(bf16[64,8,512]{2,1,0:T(8,128)(2,1)} %param.7) | copy-start | bytes 1572868
Sparse Core Ops, SparseCore 0:
  193.2 31.0 all-gather.1
  454.0 25.5 reduce-scatter.1
  482.4 698.3 all-reduce.2
where the time goes:
time: 1190 us
  waiting for transfers between devices  728 us (61%)
  blocking collectives  260 us (22%)
  matrix products  75.3 us (6%)
  starting transfers between devices  55.3 us (5%)
  local copies, waits for them, and re-layouts  35.4 us (3%)
  other arithmetic  19.9 us (2%)
  between operations  14.7 us (1%)
    unnamed x4, waiting for transfers between devices  618 us
    all_gather x1, blocking collectives, shards(): w_part = lax.all_gather(weights, 'trk', axis=2, tiled=True)  184 us
    psum x1, blocking collectives, shards(): gain_sum = lax.psum(gain_term, ('grp', 'trk'))  76.2 us
  transfers between devices with their start and end apart: 10, of which 9 were waited for; matrix products, arithmetic and copies ran while one was open for 4% of the time, Pallas kernels for 0%

commit v1 on v0

--- a/solution.py
+++ b/solution.py
@@ -109,7 +109,10 @@
 
 
 def shards(fields, upstream, ln_gain, weights):
-    w_part = lax.all_gather(weights, "trk", axis=2, tiled=True)
+    n_dev = lax.axis_size("trk")
+    shards_2 = jnp.stack([weights for _ in range(n_dev)])
+    shards_2 = lax.all_to_all(shards_2, "trk", split_axis=0, concat_axis=0)
+    w_part = jnp.concatenate(shards_2, axis=2)
     w_full = lax.all_gather(w_part, "grp", axis=1, tiled=True)
     w_in = w_full[:3]
     w_out = w_full[3]

time: 1190 us -> 1040 us (0.87)
  blocking collectives: 260 us -> 109 us
    all_gather x1 -> x0, blocking collectives: 184 us -> none  [shards(): w_part = lax.all_gather(weights, 'trk', axis=2, tiled=True)]
    all_to_all x0 -> x1, blocking collectives: none -> 33 us  [shards(): shards_2 = lax.all_to_all(shards_2, 'trk', split_axis=0, concat_axis=0)]
where the time goes in v1:
time: 1040 us
  waiting for transfers between devices  730 us (70%)
  blocking collectives  109 us (10%)
  matrix products  75.1 us (7%)
  starting transfers between devices  52.2 us (5%)
  local copies, waits for them, and re-layouts  34.6 us (3%)
  other arithmetic  21 us (2%)
  between operations  14.7 us (1%)
    unnamed x4, waiting for transfers between devices  617 us
    psum x1, blocking collectives, shards(): gain_sum = lax.psum(gain_term, ('grp', 'trk'))  76.3 us
    all_to_all x1, blocking collectives, shards(): shards_2 = lax.all_to_all(shards_2, 'trk', split_axis=0, concat_axis=0)  33 us
    all_gather x1, waiting for transfers between devices, shards(): w_full = lax.all_gather(w_part, 'grp', axis=1, tiled=True)  23.9 us
    reduce_scatter x1, waiting for transfers between devices, shards(): lax.psum_scatter(raw_grad.astype(jnp.bfloat16), 'grp', scatter_dimension=...  22.4 us
  transfers between devices with their start and end apart: 10, of which 9 were waited for; matrix products, arithmetic and copies ran while one was open for 4% of the time, Pallas kernels for 0%

profile of v1, /device:TPU:2, one launch (start us, length us, event | category | flops | bytes accessed | tf_op | source)
XLA Modules:
  0.0 1036.5 jit_solution(13983332610390034648)
XLA Ops:
  8.0 33.0 %all_to_all.77 = bf16[64,4,128,8]{2,3,1,0:T(8,128)(2,1)S(1)} all-to-all(bf16[64,4,128,8]{2,3,1,0:T(8,128)(2,1)S(1)} %stack.25), channel_id=1, replica_groups=mesh['grp'=4,'trk'=64] {'trk'}, dimensions={0} | all-to-all | bytes 1048576 | tf_op jit(solution)/shard_map/all_to_all | solution.py:114
  42.1 6.5 all-to-all-start.4
  49.1 23.9 %all-gather.2.cloned.1.call-done = bf16[4,512,512]{2,1,0:T(8,128)(2,1)} async-done(((bf16[4,128,512]{2,1,0:T(8,128)(2,1)}), bf16[4,512,512]{2,1,0:T(8,128)(2,1)}) %all-gather.2.cloned.1.call-update) | async-done | bytes 2097168 | tf_op jit(solution)/shard_map/all_gather | solution.py:116
  75.4 12.3 %all-to-all-start.1 = ((bf16[64,8,512]{2,1,0:T(8,128)(2,1)}), bf16[64,8,512]{2,1,0:T(8,128)(2,1)S(1)}, u32[]{:S(2)}, u32[]{:S(2)}) async-start(bf16[64,8,512]{2,1,0:T(8,128)(2,1)} %convolution_convert_fusion.8), calls=%async_computation.1 | async-start | bytes 1048576 | tf_op jit(solution)/shard_map/all_to_all | solution.py:124
  87.6 2.3 convolution_convert_fusion.7
  90.0 16.4 %all-to-all-done.1 = bf16[64,8,512]{2,1,0:T(8,128)(2,1)S(1)} async-done(((bf16[64,8,512]{2,1,0:T(8,128)(2,1)}), bf16[64,8,512]{2,1,0:T(8,128)(2,1)S(1)}, u32[]{:S(2)}, u32[]{:S(2)}) %all-to-all-start.1) | async-done | bytes 524320 | tf_op jit(solution)/shard_map/all_to_all | solution.py:124
  106.4 6.5 all-to-all-start.2
  112.9 2.3 convolution_convert_fusion.6
  115.3 15.6 %all-to-all-done.2 = bf16[64,8,512]{2,1,0:T(8,128)(2,1)S(1)} async-done(((bf16[64,8,512]{2,1,0:T(8,128)(2,1)}), bf16[64,8,512]{2,1,0:T(8,128)(2,1)S(1)}, u32[]{:S(2)}, u32[]{:S(2)}) %all-to-all-start.2) | async-done | bytes 524320 | tf_op jit(solution)/shard_map/all_to_all | solution.py:125
  130.8 6.7 all-to-all-start.3
  141.1 2.4 reshape.132
  144.8 9.8 all-to-all-done.3
  154.6 2.4 reshape.134
  157.0 2.3 copy.62
  159.4 60.7 %while.16 = (s32[]{:T(128)}, bf16[8,512,64]{1,2,0:T(8,128)(2,1)}, bf16[8,512,64]{1,2,0:T(8,128)(2,1)}, bf16[8,512,64]{1,2,0:T(8,128)(2,1)}, bf16[8,512,64]{1,2,0...) while((s32[]{:T(128)}, bf16[8,512,64]{1,2,0:T(8,128)(2,1)}, ...), condition=%wide.region_6.7_spmd, body=%wide.region_2.6_spmd.sunk | while | flops 206699008 | bytes 11305061 | solution.py:78
  220.1 2.4 copy.65
  223.0 3.8 reduce.1
  227.8 6.5 all-to-all-start.7
  234.4 2.4 copy.64
  236.8 3.8 reduce.2
  241.6 9.4 all-to-all-done.7
  251.1 6.7 all-to-all-start.6
  257.8 2.4 copy.63
  260.2 3.8 reduce.3
  267.8 6.1 all-to-all-done.6
  274.0 6.6 all-to-all-start.5
  282.4 3.6 reshape.159
  287.5 8.8 all-to-all-done.5
  305.1 22.4 %reduce-scatter.2.cloned.1.call-done = bf16[4,128,512]{2,1,0:T(8,128)(2,1)} async-done(((bf16[4,512,512]{2,1,0:T(8,128)(2,1)}), bf16[4,128,512]{2,1,0:T(8,128)(2,1)}) %reduce-scatter.2.cloned.1.call-update) | async-done | bytes 524304 | tf_op jit(solution)/shard_map/reduce_scatter | solution.py:145
  329.7 2.6 fusion.64
  332.4 76.3 %psum.7 = f32[512]{0:T(512)S(1)} all-reduce(f32[512]{0:T(512)S(1)} %get-tuple-element.108), channel_id=1, replica_groups=mesh['grp'=4,'trk'=64] {'grp','trk'}, use_global_device_ids=true, to_apply=%region_12.13 | all-reduce | flops 512 | bytes 4096 | tf_op jit(solution)/shard_map/psum | solution.py:149
  411.5 617.1 %all-reduce.3.cloned.1.call-done = f32[4,128,512]{1,0,2:T(4,128)} async-done(((f32[4,128,512]{1,0,2:T(4,128)}), f32[4,128,512]{1,0,2:T(4,128)}) %all-reduce.3.cloned.1.call-update) | async-done | bytes 1048592
  (127 shorter events, 94.3 us)
Async XLA Ops:
  7.2 65.9 %all-gather.2.cloned.1.call-start = ((), (), s32[]{:S(2)}) async-start(), calls=%async_computation.9 | async-start | bytes 2621440 | tf_op jit(solution)/shard_map/all_gather | solution.py:116
  41.0 7.6 copy-start
  41.1 32.0 %copy-start.7 = (f32[512]{0:T(512)S(1)}, f32[512]{0:T(512)}, u32[]{:S(2)}) copy-start(f32[512]{0:T(512)} %param.8) | copy-start | bytes 6148
  42.1 33.2 %all-to-all-start.4 = ((bf16[64,8,512]{2,1,0:T(8,128)(2,1)}), bf16[64,8,512]{2,1,0:T(8,128)(2,1)S(1)}, u32[]{:S(2)}, u32[]{:S(2)}) async-start(bf16[64,8,512]{2,1,0:T(8,128)(2,1)} %param.7), calls=%async_computation.4 | async-start | bytes 1048576 | tf_op jit(solution)/shard_map/all_to_all | solution.py:127
  75.4 31.0 %all-to-all-start.1 = ((bf16[64,8,512]{2,1,0:T(8,128)(2,1)}), bf16[64,8,512]{2,1,0:T(8,128)(2,1)S(1)}, u32[]{:S(2)}, u32[]{:S(2)}) async-start(bf16[64,8,512]{2,1,0:T(8,128)(2,1)} %convolution_convert_fusion.8), calls=%async_computation.1 | async-start | bytes 1048576 | tf_op jit(solution)/shard_map/all_to_all | solution.py:124
  106.4 24.4 %all-to-all-start.2 = ((bf16[64,8,512]{2,1,0:T(8,128)(2,1)}), bf16[64,8,512]{2,1,0:T(8,128)(2,1)S(1)}, u32[]{:S(2)}, u32[]{:S(2)}) async-start(bf16[64,8,512]{2,1,0:T(8,128)(2,1)} %convolution_convert_fusion.7), calls=%async_computation.2 | async-start | bytes 1048576 | tf_op jit(solution)/shard_map/all_to_all | solution.py:125
  130.8 9.6 copy-start.2
  130.8 23.8 %all-to-all-start.3 = ((bf16[64,8,512]{2,1,0:T(8,128)(2,1)}), bf16[64,8,512]{2,1,0:T(8,128)(2,1)}, u32[]{:S(2)}, u32[]{:S(2)}) async-start(bf16[64,8,512]{2,1,0:T(8,128)(2,1)} %convolution_convert_fusion.6), calls=%async_computation.3 | async-start | bytes 1048576 | tf_op jit(solution)/shard_map/all_to_all | solution.py:126
  227.8 23.2 %all-to-all-start.7 = ((bf16[64,2,2048]{2,1,0:T(2,128)(2,1)}), bf16[64,2,2048]{2,1,0:T(2,128)(2,1)S(1)}, u32[]{:S(2)}, u32[]{:S(2)}) async-start(bf16[64,2,2048]{2,1,0:T(2,128)(2,1)} %reshape.156), calls=%async_computation.7 | async-start | bytes 1048576 | tf_op jit(solution)/shard_map/all_to_all | solution.py:135
  251.1 22.9 %all-to-all-start.6 = ((bf16[64,2,2048]{2,1,0:T(2,128)(2,1)}), bf16[64,2,2048]{2,1,0:T(2,128)(2,1)}, u32[]{:S(2)}, u32[]{:S(2)}) async-start(bf16[64,2,2048]{2,1,0:T(2,128)(2,1)} %reshape.158), calls=%async_computation.6 | async-start | bytes 1048576 | tf_op jit(solution)/shard_map/all_to_all | solution.py:134
  274.0 22.3 %all-to-all-start.5 = ((bf16[64,2,2048]{2,1,0:T(2,128)(2,1)}), bf16[64,2,2048]{2,1,0:T(2,128)(2,1)S(1)}, u32[]{:S(2)}, u32[]{:S(2)}) async-start(bf16[64,2,2048]{2,1,0:T(2,128)(2,1)} %reshape.160), calls=%async_computation.5 | async-start | bytes 1048576 | tf_op jit(solution)/shard_map/all_to_all | solution.py:133
  280.6 46.9 %reduce-scatter.2.cloned.1.call-start = ((), (), s32[]{:S(2)}) async-start(), calls=%async_computation.10 | async-start | bytes 2621440 | tf_op jit(solution)/shard_map/reduce_scatter | solution.py:145
  298.1 2.0 copy-start.3
  298.1 2.0 copy-start.5
  298.1 2.0 copy-start.6
  301.7 0.7 copy-start.8
  301.8 726.8 %all-reduce.3.cloned.1.call-start = ((), (), s32[]{:S(2)}) async-start(), calls=%async_computation.11 | async-start | bytes 2097152
  303.6 1.3 copy-start.1
  305.0 24.8 %copy-start.4 = (bf16[1,512,512]{2,1,0:T(8,128)(2,1)S(1)}, bf16[1,512,512]{2,1,0:T(8,128)(2,1)}, u32[]{:S(2)}) copy-start(bf16[1,512,512]{2,1,0:T(8,128)(2,1)} %copy.96) | copy-start | bytes 1572868
Sparse Core Ops, SparseCore 0:
  42.2 30.7 all-gather.1
  301.9 25.5 reduce-scatter.1
  330.3 698.2 all-reduce.2
